TPU v7x, 256 devices: a whole 4x4x8 slice. The times are simulated.
256 devices in a mesh: section: 16 (over z, core), tensor: 16 (over y, x).
Axes of the slice: x: 4, y: 4, z: 8, core: 2. Of those that a mesh axis runs over, the one named last changes fastest.
Arguments:
- stream: float32 [16, 512, 8192], P('section', None, 'tensor'), may hold values from -40 to 40
- down_factor: bfloat16 [2, 16, 8192, 512], P(None, 'section', 'tensor'), may hold values from -0.0625 to 0.0625
- router: bfloat16 [2, 16, 8192, 512], P(None, 'section', 'tensor'), may hold values from -0.0625 to 0.0625
- expert_factor: bfloat16 [2, 16, 512, 32], P(None, 'section'), may hold values from -0.25 to 0.25
- core_tensor: bfloat16 [2, 16, 512, 32, 512], P(None, 'section', 'tensor'), may hold values from -0.046875 to 0.046875
- up_factor: bfloat16 [2, 16, 512, 8192], P(None, 'section', None, 'tensor'), may hold values from -0.25 to 0.25
Outputs:
- stream_out: float32 [16, 512, 8192], P('section', None, 'tensor')
All inputs are finite; a program needn't handle non-finite values.
Results may differ from a plain program's by a relative error of at most 0.0095.
Values may be sent and summed in bfloat16 or wider, within the bound.
A program may use at most 64 MiB of HBM per device.

v0:
```python
import jax
import jax.numpy as jnp
from jax import lax
from jax.sharding import PartitionSpec as P

D = 8192
TICKS = 6


EPSILON = 1e-05


def in_blocks(array, dim, peers):
    before, after = (array.shape[:dim], array.shape[dim + 1 :])
    return jnp.moveaxis(array.reshape(*before, peers, -1, *after), dim, 0)


def sent_and_summed(array, axis, dim):
    peers = lax.axis_size(axis)
    pieces = lax.all_to_all(in_blocks(array, dim, peers), axis, 0, 0, tiled=True)
    return jnp.sum(pieces, axis=0)


def sent_together(arrays, axis, dim, along):
    both = jnp.concatenate(arrays, axis=along)
    out, at, finished = (sent_and_summed(both, axis, dim), 0, [])
    for a in arrays:
        finished.append(lax.slice_in_dim(out, at, at + a.shape[along], axis=along))
        at += a.shape[along]
    return tuple(finished)


def joined_along(pieces, dim):
    pieces = jnp.moveaxis(pieces, 0, dim)
    lengths = pieces.shape
    return pieces.reshape(*lengths[:dim], lengths[dim] * lengths[dim + 1], *lengths[dim + 2 :])


def sent_to_all(array, axis):
    peers = lax.axis_size(axis)
    return lax.all_to_all(
        jnp.broadcast_to(array[None], (peers, *array.shape)), axis, 0, 0, tiled=True
    )


def gather_directly(array, axis, dim):
    return joined_along(sent_to_all(array, axis), dim)


def side_by_side(arrays, axis, dim, along):
    ends, at = ([], 0)
    for a in arrays[:-1]:
        at += a.shape[along]
        ends.append(at)
    both = jnp.concatenate(arrays, axis=along)
    return tuple(jnp.split(gather_directly(both, axis, dim), ends, axis=along))


def from_behind(value, axis, steps):
    count = lax.axis_size(axis)
    pairs = [(source, (source + steps) % count) for source in range(count)]
    return lax.ppermute(value, axis, pairs)


def select_lap(stacked, lap_id):
    return lax.dynamic_index_in_dim(stacked[:, 0], lap_id, 0, keepdims=False)


def finish_rows(projected, logits, squares, expert_part):
    factor = lax.rsqrt(squares / D + EPSILON)
    reduced = (projected * factor).astype(jnp.bfloat16)
    gating = jax.nn.sigmoid(logits * factor).astype(jnp.bfloat16)
    mixing = jnp.dot(gating, expert_part, preferred_element_type=jnp.float32).astype(jnp.bfloat16)
    return (reduced, mixing)


def core_rows(reduced, mixing, core_part):
    flattened = core_part.reshape(core_part.shape[0] * core_part.shape[1], core_part.shape[2])
    partial_value = lax.dot_general(
        reduced, flattened, (((1,), (1,)), ((), ())), preferred_element_type=jnp.float32
    )
    partial_value = partial_value.reshape(reduced.shape[0], core_part.shape[0], core_part.shape[1])
    return jnp.sum(partial_value * mixing.astype(jnp.float32)[:, None, :], axis=2).astype(
        jnp.bfloat16
    )


def per_device(stream, down_factor, router, expert_factor, core_tensor, up_factor):
    section_id = lax.axis_index("section")
    sections = lax.axis_size("section")
    front_edge = sections // 2
    carried = stream[0]
    for tick_index in range(TICKS):
        anchor = (section_id - tick_index) % sections
        lap_id = (anchor < front_edge).astype(jnp.int32) + (section_id < tick_index).astype(
            jnp.int32
        )
        down_part = select_lap(down_factor, lap_id)
        router_part = select_lap(router, lap_id)
        expert_part = select_lap(expert_factor, lap_id)
        core_part = select_lap(core_tensor, lap_id)
        up_part = select_lap(up_factor, lap_id)
        lowered = carried.astype(jnp.bfloat16)
        projected = jnp.dot(lowered, down_part, preferred_element_type=jnp.float32)
        logits = jnp.dot(lowered, router_part, preferred_element_type=jnp.float32)
        squares = jnp.sum(carried * carried, axis=1, keepdims=True)
        projected, logits, squares = sent_together((projected, logits, squares), "tensor", 0, 1)
        reduced, mixing = finish_rows(projected, logits, squares, expert_part)
        pieces = side_by_side((reduced, mixing), "tensor", 0, 1)
        ranked = core_rows(pieces[0], pieces[1], core_part)
        update = jnp.dot(
            gather_directly(ranked, "tensor", 1), up_part, preferred_element_type=jnp.float32
        )
        carried = from_behind(carried + update, "section", 1)
    return carried[None]


def solution(mesh):
    return jax.shard_map(
        per_device,
        mesh=mesh,
        in_specs=(
            P("section", None, "tensor"),
            P(None, "section", "tensor", None),
            P(None, "section", "tensor", None),
            P(None, "section", None, None),
            P(None, "section", "tensor", None, None),
            P(None, "section", None, "tensor"),
        ),
        out_specs=P("section", None, "tensor"),
        check_vma=False,
    )
```

profile of v0, /device:TPU:1, one launch (start us, length us, event | category | flops | bytes accessed | tf_op | source)
XLA Modules:
  0.0 545.3 jit_solution(16610654672556060894)
XLA Ops:
  1.5 2.9 fusion.41
  6.0 1.8 pad_maximum_fusion
  7.8 37.9 %all_to_all.90 = f32[16,32,1025]{2,1,0:T(8,128)} all-to-all(f32[16,32,1025]{2,1,0:T(8,128)S(1)} %pad_maximum_fusion), channel_id=1, replica_groups=mesh['section'=16,'tensor'=16] {'tensor'}, dimensions={0} | all-to-all | bytes 4198400 | tf_op jit(solution)/shard_map/all_to_all | solution.py:20
  45.7 1.8 reduce_sum.163
  48.0 14.6 %all_to_all.91 = bf16[16,32,544]{2,1,0:T(8,128)(2,1)S(1)} all-to-all(bf16[16,32,544]{2,1,0:T(8,128)(2,1)S(1)} %broadcast_in_dim.26), channel_id=1, replica_groups=mesh['section'=16,'tensor'=16] {'tensor'}, dimensions={0} | all-to-all | bytes 1114112 | tf_op jit(solution)/shard_map/all_to_all | solution.py:41
  63.5 1.9 multiply_reduce_fusion.5
  65.5 11.7 %all_to_all.92 = bf16[16,512,32]{1,2,0:T(8,128)(2,1)S(1)} all-to-all(bf16[16,512,32]{1,2,0:T(8,128)(2,1)S(1)} %broadcast_in_dim.27), channel_id=1, replica_groups=mesh['section'=16,'tensor'=16] {'tensor'}, dimensions={0} | all-to-all | bytes 1048576 | tf_op jit(solution)/shard_map/all_to_all | solution.py:41
  78.6 5.5 %collective-permute-start = (f32[512,512]{1,0:T(8,128)}, f32[512,512]{1,0:T(8,128)}, u32[]{:S(2)}, u32[]{:S(2)}) collective-permute-start(f32[512,512]{1,0:T(8,128)} %convolution_add_fusion.5), channel_id=1, source_target_pairs={{0,16},{16,32},{32,48},{48,64},{64,80},{80,96},{96,112},{112,128},... | collective-permute-start | bytes 3145736 | tf_op jit(solution)/shard_map/ppermute | solution.py:62
  84.1 12.1 %collective-permute-done = f32[512,512]{1,0:T(8,128)} collective-permute-done((f32[512,512]{1,0:T(8,128)}, f32[512,512]{1,0:T(8,128)}, u32[]{:S(2)}, u32[]{:S(2)}) %collective-permute-start) | collective-permute-done | bytes 1048608 | tf_op jit(solution)/shard_map/ppermute | solution.py:62
  97.9 2.5 fusion.31
  102.0 1.8 pad_maximum_fusion.1
  103.8 33.3 %all_to_all.93 = f32[16,32,1025]{2,1,0:T(8,128)} all-to-all(f32[16,32,1025]{2,1,0:T(8,128)S(1)} %pad_maximum_fusion.1), channel_id=1, replica_groups=mesh['section'=16,'tensor'=16] {'tensor'}, dimensions={0} | all-to-all | bytes 4198400 | tf_op jit(solution)/shard_map/all_to_all | solution.py:20
  137.1 1.8 reduce_sum.166
  139.4 12.4 %all_to_all.94 = bf16[16,32,544]{2,1,0:T(8,128)(2,1)S(1)} all-to-all(bf16[16,32,544]{2,1,0:T(8,128)(2,1)S(1)} %broadcast_in_dim.28), channel_id=1, replica_groups=mesh['section'=16,'tensor'=16] {'tensor'}, dimensions={0} | all-to-all | bytes 1114112 | tf_op jit(solution)/shard_map/all_to_all | solution.py:41
  152.7 11.7 %all_to_all.95 = bf16[16,512,32]{1,2,0:T(8,128)(2,1)S(1)} all-to-all(bf16[16,512,32]{1,2,0:T(8,128)(2,1)S(1)} %broadcast_in_dim.29), channel_id=1, replica_groups=mesh['section'=16,'tensor'=16] {'tensor'}, dimensions={0} | all-to-all | bytes 1048576 | tf_op jit(solution)/shard_map/all_to_all | solution.py:41
  164.4 2.8 convolution_add_fusion.4
  167.2 8.0 %collective-permute-start.1 = (f32[512,512]{1,0:T(8,128)}, f32[512,512]{1,0:T(8,128)}, u32[]{:S(2)}, u32[]{:S(2)}) collective-permute-start(f32[512,512]{1,0:T(8,128)} %convolution_add_fusion.4), channel_id=1, source_target_pairs={{0,16},{16,32},{32,48},{48,64},{64,80},{80,96},{96,112},{112,128},... | collective-permute-start | bytes 3145736 | tf_op jit(solution)/shard_map/ppermute | solution.py:62
  175.2 12.1 %collective-permute-done.1 = f32[512,512]{1,0:T(8,128)} collective-permute-done((f32[512,512]{1,0:T(8,128)}, f32[512,512]{1,0:T(8,128)}, u32[]{:S(2)}, u32[]{:S(2)}) %collective-permute-start.1) | collective-permute-done | bytes 1048608 | tf_op jit(solution)/shard_map/ppermute | solution.py:62
  192.0 1.8 pad_maximum_fusion.2
  193.8 32.9 %all_to_all.96 = f32[16,32,1025]{2,1,0:T(8,128)} all-to-all(f32[16,32,1025]{2,1,0:T(8,128)S(1)} %pad_maximum_fusion.2), channel_id=1, replica_groups=mesh['section'=16,'tensor'=16] {'tensor'}, dimensions={0} | all-to-all | bytes 4198400 | tf_op jit(solution)/shard_map/all_to_all | solution.py:20
  226.7 1.8 reduce_sum.169
  229.0 12.7 %all_to_all.97 = bf16[16,32,544]{2,1,0:T(8,128)(2,1)S(1)} all-to-all(bf16[16,32,544]{2,1,0:T(8,128)(2,1)S(1)} %broadcast_in_dim.30), channel_id=1, replica_groups=mesh['section'=16,'tensor'=16] {'tensor'}, dimensions={0} | all-to-all | bytes 1114112 | tf_op jit(solution)/shard_map/all_to_all | solution.py:41
  242.7 1.9 multiply_reduce_fusion.3
  244.6 11.7 %all_to_all.98 = bf16[16,512,32]{1,2,0:T(8,128)(2,1)S(1)} all-to-all(bf16[16,512,32]{1,2,0:T(8,128)(2,1)S(1)} %broadcast_in_dim.31), channel_id=1, replica_groups=mesh['section'=16,'tensor'=16] {'tensor'}, dimensions={0} | all-to-all | bytes 1048576 | tf_op jit(solution)/shard_map/all_to_all | solution.py:41
  256.4 2.7 convolution_add_fusion.3
  259.0 8.2 %collective-permute-start.2 = (f32[512,512]{1,0:T(8,128)}, f32[512,512]{1,0:T(8,128)}, u32[]{:S(2)}, u32[]{:S(2)}) collective-permute-start(f32[512,512]{1,0:T(8,128)} %convolution_add_fusion.3), channel_id=1, source_target_pairs={{0,16},{16,32},{32,48},{48,64},{64,80},{80,96},{96,112},{112,128},... | collective-permute-start | bytes 3145736 | tf_op jit(solution)/shard_map/ppermute | solution.py:62
  267.2 12.1 %collective-permute-done.2 = f32[512,512]{1,0:T(8,128)} collective-permute-done((f32[512,512]{1,0:T(8,128)}, f32[512,512]{1,0:T(8,128)}, u32[]{:S(2)}, u32[]{:S(2)}) %collective-permute-start.2) | collective-permute-done | bytes 1048608 | tf_op jit(solution)/shard_map/ppermute | solution.py:62
  285.8 33.9 %all_to_all.99 = f32[16,32,1025]{2,1,0:T(8,128)} all-to-all(f32[16,32,1025]{2,1,0:T(8,128)S(1)} %pad_maximum_fusion.3), channel_id=1, replica_groups=mesh['section'=16,'tensor'=16] {'tensor'}, dimensions={0} | all-to-all | bytes 4198400 | tf_op jit(solution)/shard_map/all_to_all | solution.py:20
  319.7 1.8 reduce_sum.172
  322.0 14.6 %all_to_all.100 = bf16[16,32,544]{2,1,0:T(8,128)(2,1)S(1)} all-to-all(bf16[16,32,544]{2,1,0:T(8,128)(2,1)S(1)} %broadcast_in_dim.32), channel_id=1, replica_groups=mesh['section'=16,'tensor'=16] {'tensor'}, dimensions={0} | all-to-all | bytes 1114112 | tf_op jit(solution)/shard_map/all_to_all | solution.py:41
  337.5 1.9 multiply_reduce_fusion.2
  339.4 12.1 %all_to_all.101 = bf16[16,512,32]{1,2,0:T(8,128)(2,1)S(1)} all-to-all(bf16[16,512,32]{1,2,0:T(8,128)(2,1)S(1)} %broadcast_in_dim.33), channel_id=1, replica_groups=mesh['section'=16,'tensor'=16] {'tensor'}, dimensions={0} | all-to-all | bytes 1048576 | tf_op jit(solution)/shard_map/all_to_all | solution.py:41
  351.5 2.7 convolution_add_fusion.2
  354.2 9.0 %collective-permute-start.3 = (f32[512,512]{1,0:T(8,128)}, f32[512,512]{1,0:T(8,128)}, u32[]{:S(2)}, u32[]{:S(2)}) collective-permute-start(f32[512,512]{1,0:T(8,128)} %convolution_add_fusion.2), channel_id=1, source_target_pairs={{0,16},{16,32},{32,48},{48,64},{64,80},{80,96},{96,112},{112,128},... | collective-permute-start | bytes 3145736 | tf_op jit(solution)/shard_map/ppermute | solution.py:62
  363.2 12.1 %collective-permute-done.3 = f32[512,512]{1,0:T(8,128)} collective-permute-done((f32[512,512]{1,0:T(8,128)}, f32[512,512]{1,0:T(8,128)}, u32[]{:S(2)}, u32[]{:S(2)}) %collective-permute-start.3) | collective-permute-done | bytes 1048608 | tf_op jit(solution)/shard_map/ppermute | solution.py:62
  381.8 33.5 %all_to_all.102 = f32[16,32,1025]{2,1,0:T(8,128)} all-to-all(f32[16,32,1025]{2,1,0:T(8,128)S(1)} %pad_maximum_fusion.4), channel_id=1, replica_groups=mesh['section'=16,'tensor'=16] {'tensor'}, dimensions={0} | all-to-all | bytes 4198400 | tf_op jit(solution)/shard_map/all_to_all | solution.py:20
  415.3 1.8 reduce_sum.175
  417.6 15.4 %all_to_all.103 = bf16[16,32,544]{2,1,0:T(8,128)(2,1)S(1)} all-to-all(bf16[16,32,544]{2,1,0:T(8,128)(2,1)S(1)} %broadcast_in_dim.34), channel_id=1, replica_groups=mesh['section'=16,'tensor'=16] {'tensor'}, dimensions={0} | all-to-all | bytes 1114112 | tf_op jit(solution)/shard_map/all_to_all | solution.py:41
  434.0 1.9 multiply_reduce_fusion.1
  435.9 13.1 %all_to_all.104 = bf16[16,512,32]{1,2,0:T(8,128)(2,1)S(1)} all-to-all(bf16[16,512,32]{1,2,0:T(8,128)(2,1)S(1)} %broadcast_in_dim.35), channel_id=1, replica_groups=mesh['section'=16,'tensor'=16] {'tensor'}, dimensions={0} | all-to-all | bytes 1048576 | tf_op jit(solution)/shard_map/all_to_all | solution.py:41
  449.1 2.7 convolution_add_fusion.1
  451.7 12.1 %collective-permute-done.4 = f32[512,512]{1,0:T(8,128)} collective-permute-done((f32[512,512]{1,0:T(8,128)}, f32[512,512]{1,0:T(8,128)}, u32[]{:S(2)}, u32[]{:S(2)}) %collective-permute-start.4) | collective-permute-done | bytes 1048608 | tf_op jit(solution)/shard_map/ppermute | solution.py:62
  470.0 28.9 %all_to_all.105 = f32[16,32,1025]{2,1,0:T(8,128)} all-to-all(f32[16,32,1025]{2,1,0:T(8,128)S(1)} %pad_maximum_fusion.5), channel_id=1, replica_groups=mesh['section'=16,'tensor'=16] {'tensor'}, dimensions={0} | all-to-all | bytes 4198400 | tf_op jit(solution)/shard_map/all_to_all | solution.py:20
  498.9 1.8 reduce_sum.178
  501.2 12.7 %all_to_all.106 = bf16[16,32,544]{2,1,0:T(8,128)(2,1)S(1)} all-to-all(bf16[16,32,544]{2,1,0:T(8,128)(2,1)S(1)} %broadcast_in_dim.36), channel_id=1, replica_groups=mesh['section'=16,'tensor'=16] {'tensor'}, dimensions={0} | all-to-all | bytes 1114112 | tf_op jit(solution)/shard_map/all_to_all | solution.py:41
  514.8 11.8 %all_to_all.107 = bf16[16,512,32]{1,2,0:T(8,128)(2,1)S(1)} all-to-all(bf16[16,512,32]{1,2,0:T(8,128)(2,1)S(1)} %broadcast_in_dim.37), channel_id=1, replica_groups=mesh['section'=16,'tensor'=16] {'tensor'}, dimensions={0} | all-to-all | bytes 1048576 | tf_op jit(solution)/shard_map/all_to_all | solution.py:41
  528.3 4.3 collective-permute-start.5
  532.6 11.7 %collective-permute-done.5 = f32[512,512]{1,0:T(8,128)S(1)} collective-permute-done((f32[512,512]{1,0:T(8,128)S(1)}, f32[512,512]{1,0:T(8,128)S(1)}, u32[]{:S(2)}, u32[]{:S(2)}) %collective-permute-start.5) | collective-permute-done | bytes 1048608 | tf_op jit(solution)/shard_map/ppermute | solution.py:62
  (127 shorter events, 43.1 us)
Async XLA Ops:
  0.0 63.5 %copy-start = (bf16[2,1,32,32,512]{4,3,2,1,0:T(8,128)(2,1)S(1)}, bf16[2,1,32,32,512]{4,3,2,1,0:T(8,128)(2,1)}, u32[]{:S(2)}) copy-start(bf16[2,1,32,32,512]{4,3,2,1,0:T(8,128)(2,1)} %param.10) | copy-start | bytes 6291460
  0.0 4.4 copy-start.1
  1.5 2.9 copy-start.3
  45.7 2.0 copy-start.20
  62.6 0.8 copy-start.16
  63.5 13.6 %copy-start.9 = (bf16[2,1,512,512]{3,2,1,0:T(8,128)(2,1)S(1)}, bf16[2,1,512,512]{3,2,1,0:T(8,128)(2,1)}, u32[]{:S(2)}) copy-start(bf16[2,1,512,512]{3,2,1,0:T(8,128)(2,1)} %param.11) | copy-start | bytes 3145732
  78.6 21.8 %copy-start.4 = (bf16[2,1,512,512]{3,2,1,0:T(8,128)(2,1)S(1)}, bf16[2,1,512,512]{3,2,1,0:T(8,128)(2,1)}, u32[]{:S(2)}) copy-start(bf16[2,1,512,512]{3,2,1,0:T(8,128)(2,1)} %param.8) | copy-start | bytes 3145732
  78.6 17.6 %collective-permute-start = (f32[512,512]{1,0:T(8,128)}, f32[512,512]{1,0:T(8,128)}, u32[]{:S(2)}, u32[]{:S(2)}) collective-permute-start(f32[512,512]{1,0:T(8,128)} %convolution_add_fusion.5), channel_id=1, source_target_pairs={{0,16},{16,32},{32,48},{48,64},{64,80},{80,96},{96,112},{112,128},... | collective-permute-start | bytes 3145736 | tf_op jit(solution)/shard_map/ppermute | solution.py:62
  151.9 12.5 %copy-start.10 = (bf16[2,1,512,512]{3,2,1,0:T(8,128)(2,1)S(1)}, bf16[2,1,512,512]{3,2,1,0:T(8,128)(2,1)}, u32[]{:S(2)}) copy-start(bf16[2,1,512,512]{3,2,1,0:T(8,128)(2,1)} %param.11) | copy-start | bytes 3145732
  164.4 24.5 %copy-start.2 = (bf16[2,1,512,512]{3,2,1,0:T(8,128)(2,1)S(1)}, bf16[2,1,512,512]{3,2,1,0:T(8,128)(2,1)}, u32[]{:S(2)}) copy-start(bf16[2,1,512,512]{3,2,1,0:T(8,128)(2,1)} %param.7) | copy-start | bytes 3145732
  167.2 20.1 %collective-permute-start.1 = (f32[512,512]{1,0:T(8,128)}, f32[512,512]{1,0:T(8,128)}, u32[]{:S(2)}, u32[]{:S(2)}) collective-permute-start(f32[512,512]{1,0:T(8,128)} %convolution_add_fusion.4), channel_id=1, source_target_pairs={{0,16},{16,32},{32,48},{48,64},{64,80},{80,96},{96,112},{112,128},... | collective-permute-start | bytes 3145736 | tf_op jit(solution)/shard_map/ppermute | solution.py:62
  175.2 15.2 %copy-start.5 = (bf16[2,1,512,512]{3,2,1,0:T(8,128)(2,1)S(1)}, bf16[2,1,512,512]{3,2,1,0:T(8,128)(2,1)}, u32[]{:S(2)}) copy-start(bf16[2,1,512,512]{3,2,1,0:T(8,128)(2,1)} %param.8) | copy-start | bytes 3145732
  241.7 0.8 copy-start.17
  242.7 13.7 %copy-start.11 = (bf16[2,1,512,512]{3,2,1,0:T(8,128)(2,1)S(1)}, bf16[2,1,512,512]{3,2,1,0:T(8,128)(2,1)}, u32[]{:S(2)}) copy-start(bf16[2,1,512,512]{3,2,1,0:T(8,128)(2,1)} %param.11) | copy-start | bytes 3145732
  259.0 20.2 %collective-permute-start.2 = (f32[512,512]{1,0:T(8,128)}, f32[512,512]{1,0:T(8,128)}, u32[]{:S(2)}, u32[]{:S(2)}) collective-permute-start(f32[512,512]{1,0:T(8,128)} %convolution_add_fusion.3), channel_id=1, source_target_pairs={{0,16},{16,32},{32,48},{48,64},{64,80},{80,96},{96,112},{112,128},... | collective-permute-start | bytes 3145736 | tf_op jit(solution)/shard_map/ppermute | solution.py:62
  267.2 15.2 %copy-start.6 = (bf16[2,1,512,512]{3,2,1,0:T(8,128)(2,1)S(1)}, bf16[2,1,512,512]{3,2,1,0:T(8,128)(2,1)}, u32[]{:S(2)}) copy-start(bf16[2,1,512,512]{3,2,1,0:T(8,128)(2,1)} %param.8) | copy-start | bytes 3145732
  336.5 0.8 copy-start.18
  337.5 14.0 %copy-start.12 = (bf16[2,1,512,512]{3,2,1,0:T(8,128)(2,1)S(1)}, bf16[2,1,512,512]{3,2,1,0:T(8,128)(2,1)}, u32[]{:S(2)}) copy-start(bf16[2,1,512,512]{3,2,1,0:T(8,128)(2,1)} %param.11) | copy-start | bytes 3145732
  354.2 21.1 %collective-permute-start.3 = (f32[512,512]{1,0:T(8,128)}, f32[512,512]{1,0:T(8,128)}, u32[]{:S(2)}, u32[]{:S(2)}) collective-permute-start(f32[512,512]{1,0:T(8,128)} %convolution_add_fusion.2), channel_id=1, source_target_pairs={{0,16},{16,32},{32,48},{48,64},{64,80},{80,96},{96,112},{112,128},... | collective-permute-start | bytes 3145736 | tf_op jit(solution)/shard_map/ppermute | solution.py:62
  363.2 15.2 %copy-start.7 = (bf16[2,1,512,512]{3,2,1,0:T(8,128)(2,1)S(1)}, bf16[2,1,512,512]{3,2,1,0:T(8,128)(2,1)}, u32[]{:S(2)}) copy-start(bf16[2,1,512,512]{3,2,1,0:T(8,128)(2,1)} %param.8) | copy-start | bytes 3145732
  433.0 0.8 copy-start.19
  434.0 15.1 %copy-start.13 = (bf16[2,1,512,512]{3,2,1,0:T(8,128)(2,1)S(1)}, bf16[2,1,512,512]{3,2,1,0:T(8,128)(2,1)}, u32[]{:S(2)}) copy-start(bf16[2,1,512,512]{3,2,1,0:T(8,128)(2,1)} %param.11) | copy-start | bytes 3145732
  451.7 12.1 %collective-permute-start.4 = (f32[512,512]{1,0:T(8,128)}, f32[512,512]{1,0:T(8,128)}, u32[]{:S(2)}, u32[]{:S(2)}) collective-permute-start(f32[512,512]{1,0:T(8,128)} %convolution_add_fusion.1), channel_id=1, source_target_pairs={{0,16},{16,32},{32,48},{48,64},{64,80},{80,96},{96,112},{112,128},... | collective-permute-start | bytes 3145736 | tf_op jit(solution)/shard_map/ppermute | solution.py:62
  451.7 15.2 %copy-start.8 = (bf16[2,1,512,512]{3,2,1,0:T(8,128)(2,1)S(1)}, bf16[2,1,512,512]{3,2,1,0:T(8,128)(2,1)}, u32[]{:S(2)}) copy-start(bf16[2,1,512,512]{3,2,1,0:T(8,128)(2,1)} %param.8) | copy-start | bytes 3145732
  466.9 1.6 copy-start.15
  514.0 12.6 %copy-start.14 = (bf16[2,1,512,512]{3,2,1,0:T(8,128)(2,1)S(1)}, bf16[2,1,512,512]{3,2,1,0:T(8,128)(2,1)}, u32[]{:S(2)}) copy-start(bf16[2,1,512,512]{3,2,1,0:T(8,128)(2,1)} %param.11) | copy-start | bytes 3145732
  528.3 16.0 %collective-permute-start.5 = (f32[512,512]{1,0:T(8,128)S(1)}, f32[512,512]{1,0:T(8,128)S(1)}, u32[]{:S(2)}, u32[]{:S(2)}) collective-permute-start(f32[512,512]{1,0:T(8,128)S(1)} %convolution_add_fusion), channel_id=1, source_target_pairs={{0,16},{16,32},{32,48},{48,64},{64,80},{80,96},{96,112},{112,128},... | collective-permute-start | bytes 3145736 | tf_op jit(solution)/shard_map/ppermute | solution.py:62
where the time goes:
time: 554 us; the launch traced here: 545 us
  blocking collectives  355 us (64%)
  waiting for transfers between devices  72 us (13%)
  matrix products  43.8 us (8%)
  starting transfers between devices  35 us (6%)
  other arithmetic  32.3 us (6%)
  local copies, waits for them, and re-layouts  6.73 us (1%)
    all_to_all x6, blocking collectives, sent_and_summed(): lax.all_to_all(in_blocks(array, dim, peers), axis, 0, 0, tiled=True)  200 us
    all_to_all x12, blocking collectives, sent_to_all(): lax.all_to_all(jnp.broadcast_to(array[None], (peers, *array.shape)), axis...  154 us
    ppermute x6, waiting for transfers between devices, from_behind(): return lax.ppermute(value, axis, pairs)  72 us
    ppermute x6, starting transfers between devices, from_behind(): return lax.ppermute(value, axis, pairs)  35 us
    dot_general x6, matrix products, per_device(): jnp.dot(gather_directly(ranked, 'tensor', 1), up_part, preferred_element_...  13.9 us
    dot_general x6, matrix products, per_device(): projected = jnp.dot(lowered, down_part, preferred_element_type=jnp.float32)  11.1 us
  transfers between devices with their start and end apart: 6, of which 6 were waited for; matrix products, arithmetic and copies ran while one was open for 0% of the time, Pallas kernels for 0%

commit v1 on v0

v1 whole, which is shorter than its diff:
```python
import functools

import jax
import jax.numpy as jnp
from jax import lax
from jax.experimental import pallas as pl
from jax.experimental.pallas import tpu as pltpu
from jax.sharding import PartitionSpec as P

D = 8192
TICKS = 6
EPSILON = 1e-05
MB = 512
RANK = 512
EX = 32
FB = 32
NT = 16
C = 2
T = MB // C
TB = T // NT
G = TB // 8
MESH = pl.DeviceIdType.MESH
F32 = jnp.float32
BF16 = jnp.bfloat16
NT_DIMS = (((1,), (1,)), ((), ()))
TN_DIMS = (((0,), (0,)), ((), ()))


def kernel(
    stream, down, router, expert, core, up, out,
    w_down, w_router, w_expert, w_core, w_up, expert4, selector, unpack, ones,
    h, square_own, square_in, logit_own, logit_in, proj_own, proj_in, reduced, mixing, ranked,
    load_sem, h_send, h_recv, square_send, square_recv, logit_send, logit_recv,
    proj_send, proj_recv, reduced_send, reduced_recv, mixing_send, mixing_recv, ranked_send, ranked_recv, out_sem,
):
    me = lax.axis_index("tensor")
    section = lax.axis_index("section")
    sections = lax.axis_size("section")
    after = lax.rem(section + 1, sections)
    before = lax.rem(section + sections - 1, sections)

    loads = []
    for c in range(C):
        loads.append(pltpu.make_async_copy(stream.at[0, pl.ds(c * T, T)], h.at[0, c], load_sem.at[c]))
    for i, (a, b) in enumerate(
        ((router, w_router), (down, w_down), (expert, w_expert), (core, w_core), (up, w_up))
    ):
        loads.append(pltpu.make_async_copy(a, b, load_sem.at[C + i]))
    for copy in loads:
        copy.start()

    barrier = pltpu.get_barrier_semaphore()
    for d in range(1, NT):
        pl.semaphore_signal(barrier, inc=1, device_id={"tensor": lax.rem(me + d, NT)}, device_id_type=MESH)
    pl.semaphore_signal(barrier, inc=1, device_id={"section": after}, device_id_type=MESH)
    pl.semaphore_signal(barrier, inc=1, device_id={"section": before}, device_id_type=MESH)

    ones[...] = jnp.ones((8, MB), BF16)
    rows = lax.broadcasted_iota(jnp.int32, (FB, FB * EX), 0)
    columns = lax.broadcasted_iota(jnp.int32, (FB, FB * EX), 1)
    selector[...] = jnp.where(columns // EX == rows, 1.0, 0.0).astype(BF16)
    rows = lax.broadcasted_iota(jnp.int32, (128, 128), 0)
    columns = lax.broadcasted_iota(jnp.int32, (128, 128), 1)
    for g in range(G):
        unpack[g] = jnp.where(rows == g * EX + columns % EX, 1.0, 0.0).astype(BF16)

    for copy in loads:
        copy.wait()
    for lap in range(2):
        one = w_expert[lap, 0]
        expert4[lap] = jnp.concatenate([one, one, one, one], axis=1)

    pl.semaphore_wait(barrier, NT + 1)

    def to_peers(source, target, send, recv):
        for d in range(1, NT):
            peer = lax.rem(me + d, NT)
            pltpu.make_async_remote_copy(
                source(d, peer), target(d), send, recv, device_id={"tensor": peer}, device_id_type=MESH
            ).start()

    def wait_bytes(ref, sem):
        pltpu.make_async_copy(ref, ref, sem).wait()

    def project(k, c, lap):
        x = h[k, c]

        @pl.when(k > 0)
        def _():
            wait_bytes(square_in.at[0, c], square_send.at[c])
            wait_bytes(logit_own.at[c, pl.ds(0, NT - 1)], logit_send.at[c])
            wait_bytes(proj_own.at[c, pl.ds(0, NT - 1)], proj_send.at[c])

        squares = lax.dot_general(ones[...], (x * x).astype(BF16), NT_DIMS, preferred_element_type=F32)
        square_own[c] = squares[0:1]
        to_peers(lambda d, p: square_own.at[c], lambda d: square_in.at[k, c, d - 1], square_send.at[c], square_recv.at[k, c])
        low = x.astype(BF16)
        part = jnp.dot(low, w_router[lap, 0], preferred_element_type=F32)
        logit_own[c] = part.astype(BF16).reshape(NT, TB, RANK)
        to_peers(lambda d, p: logit_own.at[c, p], lambda d: logit_in.at[k, c, d - 1], logit_send.at[c], logit_recv.at[k, c])
        part = jnp.dot(low, w_down[lap, 0], preferred_element_type=F32)
        proj_own[c] = part.astype(BF16).reshape(NT, TB, RANK)
        to_peers(lambda d, p: proj_own.at[c, p], lambda d: proj_in.at[k, c, d - 1], proj_send.at[c], proj_recv.at[k, c])

    def finish(k, c, lap):
        wait_bytes(square_in.at[k, c], square_recv.at[k, c])
        total = square_own[c]
        for d in range(NT - 1):
            total = total + square_in[k, c, d]
        at = lax.broadcasted_iota(jnp.int32, (TB, T), 1) == me * TB + lax.broadcasted_iota(jnp.int32, (TB, T), 0)
        own = jnp.sum(jnp.where(at, jnp.broadcast_to(total, (TB, T)), 0.0), axis=1, keepdims=True)
        factor = lax.rsqrt(own / D + EPSILON)

        wait_bytes(logit_in.at[k, c], logit_recv.at[k, c])
        logits = logit_own[c, me].astype(F32)
        for d in range(NT - 1):
            logits = logits + logit_in[k, c, d].astype(F32)
        gating = jax.nn.sigmoid(logits * factor).astype(BF16)
        mixed = jnp.dot(gating, expert4[lap], preferred_element_type=F32)
        mixed = mixed.astype(BF16).astype(F32)
        lane = lax.broadcasted_iota(jnp.int32, (8, 128), 1) // EX
        packed = jnp.zeros((8, 128), F32)
        for g in range(G):
            packed = jnp.where(lane == g, mixed[g * 8 : g * 8 + 8], packed)
        mixing[k, c, me] = packed
        to_peers(lambda d, p: mixing.at[k, c, me], lambda d: mixing.at[k, c, me], mixing_send.at[c], mixing_recv.at[k, c])

        wait_bytes(proj_in.at[k, c], proj_recv.at[k, c])
        projected = proj_own[c, me].astype(F32)
        for d in range(NT - 1):
            projected = projected + proj_in[k, c, d].astype(F32)
        reduced[k, c, me] = (projected * factor).astype(BF16)
        to_peers(lambda d, p: reduced.at[k, c, me], lambda d: reduced.at[k, c, me], reduced_send.at[c], reduced_recv.at[k, c])

    def core_stage(k, c, lap):
        wait_bytes(mixing.at[k, c, pl.ds(0, NT - 1)], mixing_recv.at[k, c])
        packed = mixing[k, c].reshape(128, 128).astype(BF16)
        wait_bytes(reduced.at[k, c, pl.ds(0, NT - 1)], reduced_recv.at[k, c])
        part = lax.dot_general(
            reduced[k, c].reshape(T, RANK), w_core[lap, 0].reshape(FB * EX, RANK), NT_DIMS, preferred_element_type=F32
        ).reshape(NT, G, 8, FB * EX)
        for g in range(G):
            weights = jnp.dot(packed, unpack[g], preferred_element_type=F32).reshape(NT, 8, 128)
            weights = jnp.concatenate([weights] * (FB * EX // 128), axis=2)
            product = (part[:, g] * weights).reshape(128, FB * EX).astype(BF16)
            ranked[k, c, me, :, g * 128 : g * 128 + 128] = lax.dot_general(
                selector[...], product, NT_DIMS, preferred_element_type=F32
            ).astype(BF16)
        to_peers(lambda d, p: ranked.at[k, c, me], lambda d: ranked.at[k, c, me], ranked_send.at[c], ranked_recv.at[k, c])

    def advance(k, c, lap):
        wait_bytes(ranked.at[k, c, pl.ds(0, NT - 1)], ranked_recv.at[k, c])
        update = lax.dot_general(
            ranked[k, c].reshape(RANK, T), w_up[lap, 0], TN_DIMS, preferred_element_type=F32
        )
        update = update.reshape(G, NT, 8, 512)
        for g in range(G):
            rows = h[k, c].reshape(NT, G, 8, 512)[:, g] + update[g]
            for j in range(NT):
                h[k, c, (j * G + g) * 8 : (j * G + g) * 8 + 8] = rows[j]
        pltpu.make_async_remote_copy(
            h.at[k, c], h.at[k + 1, c], h_send.at[c], h_recv.at[k + 1, c],
            device_id={"section": after}, device_id_type=MESH,
        ).start()

    def tick(k, carry):
        anchor = lax.rem(section - k + sections, sections)
        lap = jnp.where(anchor < sections // 2, 1, 0) + jnp.where(section < k, 1, 0)
        for c in range(C):

            @pl.when(k > 0)
            def _():
                wait_bytes(h.at[k, c], h_recv.at[k, c])

            project(k, c, lap)
        for c in range(C):
            finish(k, c, lap)
        for c in range(C):
            core_stage(k, c, lap)
        for c in range(C):
            advance(k, c, lap)
        return carry

    lax.fori_loop(0, TICKS, tick, 0)
    copies = []
    for c in range(C):
        wait_bytes(h.at[TICKS, c], h_recv.at[TICKS, c])
        copies.append(pltpu.make_async_copy(h.at[TICKS, c], out.at[0, pl.ds(c * T, T)], out_sem.at[c]))
        copies[-1].start()
    for c in range(C):
        wait_bytes(square_in.at[0, c], square_send.at[c])
        wait_bytes(logit_own.at[c, pl.ds(0, NT - 1)], logit_send.at[c])
        wait_bytes(proj_own.at[c, pl.ds(0, NT - 1)], proj_send.at[c])
        wait_bytes(mixing.at[:, c, pl.ds(0, NT - 1)], mixing_send.at[c])
        wait_bytes(reduced.at[:, c, pl.ds(0, NT - 1)], reduced_send.at[c])
        wait_bytes(ranked.at[:, c, pl.ds(0, NT - 1)], ranked_send.at[c])
        wait_bytes(h.at[pl.ds(0, TICKS), c], h_send.at[c])
    for copy in copies:
        copy.wait()


def per_device(stream, down_factor, router, expert_factor, core_tensor, up_factor):
    operands = (stream, down_factor, router, expert_factor, core_tensor, up_factor)
    dma = pltpu.SemaphoreType.DMA
    return pl.pallas_call(
        kernel,
        out_shape=jax.ShapeDtypeStruct(stream.shape, F32),
        in_specs=[pl.BlockSpec(memory_space=pl.ANY)] * len(operands),
        out_specs=pl.BlockSpec(memory_space=pl.ANY),
        scratch_shapes=[
            pltpu.VMEM(down_factor.shape, BF16),
            pltpu.VMEM(router.shape, BF16),
            pltpu.VMEM(expert_factor.shape, BF16),
            pltpu.VMEM(core_tensor.shape, BF16),
            pltpu.VMEM(up_factor.shape, BF16),
            pltpu.VMEM((2, RANK, 128), BF16),
            pltpu.VMEM((FB, FB * EX), BF16),
            pltpu.VMEM((G, 128, 128), BF16),
            pltpu.VMEM((8, MB), BF16),
            pltpu.VMEM((TICKS + 1, C, T, 512), F32),
            pltpu.VMEM((C, 1, T), F32),
            pltpu.VMEM((TICKS, C, NT - 1, 1, T), F32),
            pltpu.VMEM((C, NT, TB, RANK), BF16),
            pltpu.VMEM((TICKS, C, NT - 1, TB, RANK), BF16),
            pltpu.VMEM((C, NT, TB, RANK), BF16),
            pltpu.VMEM((TICKS, C, NT - 1, TB, RANK), BF16),
            pltpu.VMEM((TICKS, C, NT, TB, RANK), BF16),
            pltpu.VMEM((TICKS, C, NT, 8, 128), F32),
            pltpu.VMEM((TICKS, C, NT, FB, T), BF16),
            dma((C + 5,)),
            dma((C,)),
            dma((TICKS + 1, C)),
            dma((C,)),
            dma((TICKS, C)),
            dma((C,)),
            dma((TICKS, C)),
            dma((C,)),
            dma((TICKS, C)),
            dma((C,)),
            dma((TICKS, C)),
            dma((C,)),
            dma((TICKS, C)),
            dma((C,)),
            dma((TICKS, C)),
            dma((C,)),
        ],
        compiler_params=pltpu.CompilerParams(
            collective_id=0, has_side_effects=True, vmem_limit_bytes=60 << 20
        ),
        name="relay_window",
    )(*operands)


def solution(mesh):
    return jax.shard_map(
        per_device,
        mesh=mesh,
        in_specs=(
            P("section", None, "tensor"),
            P(None, "section", "tensor", None),
            P(None, "section", "tensor", None),
            P(None, "section", None, None),
            P(None, "section", "tensor", None, None),
            P(None, "section", None, "tensor"),
        ),
        out_specs=P("section", None, "tensor"),
        check_vma=False,
    )
```

time: 554 us -> 200 us (0.36); the launches traced: 545 us -> 198 us
  blocking collectives: 355 us -> 0 us
  Pallas kernels: 0 us -> 194 us
  waiting for transfers between devices: 72 us -> 0 us
  matrix products: 43.8 us -> 0 us
  starting transfers between devices: 35 us -> 0 us
  other arithmetic: 32.3 us -> 0 us
    all_to_all x18 -> x0, blocking collectives: 355 us -> none  [the longest x6 200 us: sent_and_summed(): lax.all_to_all(in_blocks(array, dim, peers), axis, 0, 0, tiled=True)]
    pallas_call x0 -> x1, Pallas kernels: none -> 194 us  [per_device(): pl.pallas_call(kernel, out_shape=jax.ShapeDtypeStruct(stream.shape, F32),...]
    ppermute x6 -> x0, waiting for transfers between devices: 72 us -> none  [from_behind(): return lax.ppermute(value, axis, pairs)]
    dot_general x30 -> x0, matrix products: 43.8 us -> none  [the longest x6 13.9 us: per_device(): jnp.dot(gather_directly(ranked, 'tensor', 1), up_part, preferred_element_...]
    ppermute x6 -> x0, starting transfers between devices: 35 us -> none  [from_behind(): return lax.ppermute(value, axis, pairs)]
    reduce_sum x7 -> x0, other arithmetic: 12.3 us -> none  [the longest x6 10.8 us: sent_and_summed(): return jnp.sum(pieces, axis=0)]
    concatenate x12 -> x0, other arithmetic: 10.3 us -> none  [the longest x6 10.2 us: sent_together(): both = jnp.concatenate(arrays, axis=along)]
    convert_element_type x17 -> x0, other arithmetic: 9.01 us -> none  [the longest x5 8.49 us: per_device(): lowered = carried.astype(jnp.bfloat16)]
  transfers between devices with their start and end apart: 6 -> 0, of which waited for: 6 -> 0; matrix products, arithmetic and copies ran while one was open for 0% -> 0% of each run, Pallas kernels for 0% -> 0%
where the time goes in v1:
time: 200 us; the launch traced here: 198 us
  Pallas kernels  194 us (97%)
  local copies, waits for them, and re-layouts  3.94 us (2%)
    pallas_call x1, Pallas kernels, per_device(): pl.pallas_call(kernel, out_shape=jax.ShapeDtypeStruct(stream.shape, F32),...  194 us

profile of v1, /device:TPU:1, one launch (start us, length us, event | category | flops | bytes accessed | tf_op | source)
XLA Modules:
  0.0 198.4 jit_solution(9489082172109513512)
XLA Ops:
  0.0 1.7 copy.7.expert
  1.7 194.5 %relay_window.1 = f32[1,512,512]{2,1,0:T(8,128)} custom-call(f32[1,512,512]{2,1,0:T(8,128)} %stream.1, bf16[2,1,512,512]{3,2,1,0:T(8,128)(2,1)} %down.1, bf16[2,1,512,512]{3,2,1,0:T(8,128)(2,1)} %router.1, bf16[2,1,512,32]{3,2,1,0:T(8,128)(2,1)} %copy.7.expert, bf16[2,1,32,32,512]{4,3,2,1,0:T(8,128)(2,1)} %core.1, bf16[2,1,512,512]{3,2,1,0:T(8,128)(2,1)} %up.1), custom_call_target="tpu_custom_call" | custom-call | tf_op jit(solution)/shard_map/relay_window/pallas_call | solution.py:205
  196.2 2.3 %copy.9 = f32[1,512,512]{2,1,0:T(8,128)} copy(f32[1,512,512]{2,1,0:T(8,128)} %relay_window.1) | data formatting | bytes 2097152

commit v2 on v1

--- a/solution.py
+++ b/solution.py
@@ -28,9 +28,9 @@
 
 def kernel(
     stream, down, router, expert, core, up, out,
-    w_down, w_router, w_expert, w_core, w_up, expert4, selector, unpack, ones,
-    h, square_own, square_in, logit_own, logit_in, proj_own, proj_in, reduced, mixing, ranked,
-    load_sem, h_send, h_recv, square_send, square_recv, logit_send, logit_recv,
+    w_down, w_router, w_expert, w_core, up_in, expert4, selector, unpack, ones,
+    h, square_own, square_in, logit_own, logit_in, proj_own, proj_in, reduced, mixing, ranked_own, ranked,
+    load_sem, up_send, up_recv, h_send, h_recv, square_send, square_recv, logit_send, logit_recv,
     proj_send, proj_recv, reduced_send, reduced_recv, mixing_send, mixing_recv, ranked_send, ranked_recv, out_sem,
 ):
     me = lax.axis_index("tensor")
@@ -43,17 +43,18 @@
     for c in range(C):
         loads.append(pltpu.make_async_copy(stream.at[0, pl.ds(c * T, T)], h.at[0, c], load_sem.at[c]))
     for i, (a, b) in enumerate(
-        ((router, w_router), (down, w_down), (expert, w_expert), (core, w_core), (up, w_up))
+        ((router, w_router), (down, w_down), (expert, w_expert), (core, w_core))
     ):
         loads.append(pltpu.make_async_copy(a, b, load_sem.at[C + i]))
     for copy in loads:
         copy.start()
 
     barrier = pltpu.get_barrier_semaphore()
-    for d in range(1, NT):
-        pl.semaphore_signal(barrier, inc=1, device_id={"tensor": lax.rem(me + d, NT)}, device_id_type=MESH)
-    pl.semaphore_signal(barrier, inc=1, device_id={"section": after}, device_id_type=MESH)
-    pl.semaphore_signal(barrier, inc=1, device_id={"section": before}, device_id_type=MESH)
+    for d in range(NT):
+        peer = lax.rem(me + d, NT)
+        if d:
+            pl.semaphore_signal(barrier, inc=1, device_id={"tensor": peer}, device_id_type=MESH)
+        pl.semaphore_signal(barrier, inc=1, device_id={"section": before, "tensor": peer}, device_id_type=MESH)
 
     ones[...] = jnp.ones((8, MB), BF16)
     rows = lax.broadcasted_iota(jnp.int32, (FB, FB * EX), 0)
@@ -70,7 +71,18 @@
         one = w_expert[lap, 0]
         expert4[lap] = jnp.concatenate([one, one, one, one], axis=1)
 
-    pl.semaphore_wait(barrier, NT + 1)
+    pl.semaphore_wait(barrier, 2 * NT - 1)
+
+    def lap_of(s, k):
+        return jnp.where(lax.rem(s - k + sections, sections) < sections // 2, 1, 0) + jnp.where(s < k, 1, 0)
+
+    def hand_up(lap):
+        pltpu.make_async_remote_copy(
+            up.at[lap], up_in.at[lap], up_send.at[lap], up_recv.at[lap],
+            device_id={"section": after}, device_id_type=MESH,
+        ).start()
+
+    hand_up(lap_of(section, 0))
 
     def to_peers(source, target, send, recv):
         for d in range(1, NT):
@@ -143,48 +155,66 @@
             weights = jnp.dot(packed, unpack[g], preferred_element_type=F32).reshape(NT, 8, 128)
             weights = jnp.concatenate([weights] * (FB * EX // 128), axis=2)
             product = (part[:, g] * weights).reshape(128, FB * EX).astype(BF16)
-            ranked[k, c, me, :, g * 128 : g * 128 + 128] = lax.dot_general(
+            ranked_own[k, c, :, g * 128 : g * 128 + 128] = lax.dot_general(
                 selector[...], product, NT_DIMS, preferred_element_type=F32
             ).astype(BF16)
-        to_peers(lambda d, p: ranked.at[k, c, me], lambda d: ranked.at[k, c, me], ranked_send.at[c], ranked_recv.at[k, c])
+        for d in range(NT):
+            pltpu.make_async_remote_copy(
+                ranked_own.at[k, c], ranked.at[k, c, me], ranked_send.at[c], ranked_recv.at[k, c],
+                device_id={"section": after, "tensor": lax.rem(me + d, NT)}, device_id_type=MESH,
+            ).start()
 
     def advance(k, c, lap):
-        wait_bytes(ranked.at[k, c, pl.ds(0, NT - 1)], ranked_recv.at[k, c])
+        wait_bytes(h.at[k + 1, c], h_recv.at[k + 1, c])
+        wait_bytes(ranked.at[k, c], ranked_recv.at[k, c])
         update = lax.dot_general(
-            ranked[k, c].reshape(RANK, T), w_up[lap, 0], TN_DIMS, preferred_element_type=F32
+            ranked[k, c].reshape(RANK, T), up_in[lap, 0], TN_DIMS, preferred_element_type=F32
         )
         update = update.reshape(G, NT, 8, 512)
         for g in range(G):
-            rows = h[k, c].reshape(NT, G, 8, 512)[:, g] + update[g]
+            rows = h[k + 1, c].reshape(NT, G, 8, 512)[:, g] + update[g]
             for j in range(NT):
-                h[k, c, (j * G + g) * 8 : (j * G + g) * 8 + 8] = rows[j]
+                h[k + 1, c, (j * G + g) * 8 : (j * G + g) * 8 + 8] = rows[j]
+
+    def hand_on(k, c):
         pltpu.make_async_remote_copy(
             h.at[k, c], h.at[k + 1, c], h_send.at[c], h_recv.at[k + 1, c],
             device_id={"section": after}, device_id_type=MESH,
         ).start()
 
     def tick(k, carry):
-        anchor = lax.rem(section - k + sections, sections)
-        lap = jnp.where(anchor < sections // 2, 1, 0) + jnp.where(section < k, 1, 0)
+        lap = lap_of(section, k)
+        earlier = lap_of(before, k - 1)
         for c in range(C):
 
             @pl.when(k > 0)
             def _():
-                wait_bytes(h.at[k, c], h_recv.at[k, c])
-
+                if c == 0:
+
+                    @pl.when(k < 3)
+                    def _():
+                        which = jnp.where(k == 1, lap_of(before, 0), 1 - lap_of(before, 0))
+                        wait_bytes(up_in.at[which], up_recv.at[which])
+
+                advance(k - 1, c, earlier)
+
+            hand_on(k, c)
             project(k, c, lap)
+
+        @pl.when(k == 1)
+        def _():
+            hand_up(1 - lap_of(section, 0))
+
         for c in range(C):
             finish(k, c, lap)
         for c in range(C):
             core_stage(k, c, lap)
-        for c in range(C):
-            advance(k, c, lap)
         return carry
 
     lax.fori_loop(0, TICKS, tick, 0)
     copies = []
     for c in range(C):
-        wait_bytes(h.at[TICKS, c], h_recv.at[TICKS, c])
+        advance(TICKS - 1, c, lap_of(before, TICKS - 1))
         copies.append(pltpu.make_async_copy(h.at[TICKS, c], out.at[0, pl.ds(c * T, T)], out_sem.at[c]))
         copies[-1].start()
     for c in range(C):
@@ -193,8 +223,10 @@
         wait_bytes(proj_own.at[c, pl.ds(0, NT - 1)], proj_send.at[c])
         wait_bytes(mixing.at[:, c, pl.ds(0, NT - 1)], mixing_send.at[c])
         wait_bytes(reduced.at[:, c, pl.ds(0, NT - 1)], reduced_send.at[c])
-        wait_bytes(ranked.at[:, c, pl.ds(0, NT - 1)], ranked_send.at[c])
+        wait_bytes(ranked.at[:, c], ranked_send.at[c])
         wait_bytes(h.at[pl.ds(0, TICKS), c], h_send.at[c])
+    for lap in range(2):
+        wait_bytes(up_in.at[lap], up_send.at[lap])
     for copy in copies:
         copy.wait()
 
@@ -226,8 +258,11 @@
             pltpu.VMEM((TICKS, C, NT - 1, TB, RANK), BF16),
             pltpu.VMEM((TICKS, C, NT, TB, RANK), BF16),
             pltpu.VMEM((TICKS, C, NT, 8, 128), F32),
+            pltpu.VMEM((TICKS, C, FB, T), BF16),
             pltpu.VMEM((TICKS, C, NT, FB, T), BF16),
-            dma((C + 5,)),
+            dma((C + 4,)),
+            dma((2,)),
+            dma((2,)),
             dma((C,)),
             dma((TICKS + 1, C)),
             dma((C,)),

time: 200 us -> 181 us (0.905)
  Pallas kernels: 194 us -> 177 us
    pallas_call x1, Pallas kernels: 194 us -> 177 us  [per_device(): pl.pallas_call(kernel, out_shape=jax.ShapeDtypeStruct(stream.shape, F32),...]
where the time goes in v2:
time: 181 us
  Pallas kernels  177 us (98%)
  local copies, waits for them, and re-layouts  3.94 us (2%)
    pallas_call x1, Pallas kernels, per_device(): pl.pallas_call(kernel, out_shape=jax.ShapeDtypeStruct(stream.shape, F32),...  177 us
    unnamed x2, local copies, waits for them, and re-layouts  3.94 us

profile of v2, /device:TPU:1, one launch (start us, length us, event | category | flops | bytes accessed | tf_op | source)
XLA Modules:
  0.0 180.6 jit_solution(14483117108114206444)
XLA Ops:
  0.0 1.7 copy.7.expert
  1.7 176.7 %relay_window.1 = f32[1,512,512]{2,1,0:T(8,128)} custom-call(f32[1,512,512]{2,1,0:T(8,128)} %stream.1, bf16[2,1,512,512]{3,2,1,0:T(8,128)(2,1)} %down.1, bf16[2,1,512,512]{3,2,1,0:T(8,128)(2,1)} %router.1, bf16[2,1,512,32]{3,2,1,0:T(8,128)(2,1)} %copy.7.expert, bf16[2,1,32,32,512]{4,3,2,1,0:T(8,128)(2,1)} %core.1, bf16[2,1,512,512]{3,2,1,0:T(8,128)(2,1)} %up.1), custom_call_target="tpu_custom_call" | custom-call | tf_op jit(solution)/shard_map/relay_window/pallas_call | solution.py:237
  178.4 2.3 %copy.9 = f32[1,512,512]{2,1,0:T(8,128)} copy(f32[1,512,512]{2,1,0:T(8,128)} %relay_window.1) | data formatting | bytes 2097152

commit v3 on v2

--- a/solution.py
+++ b/solution.py
@@ -15,10 +15,10 @@
 EX = 32
 FB = 32
 NT = 16
-C = 2
+C = 4
 T = MB // C
 TB = T // NT
-G = TB // 8
+RP = TB // 4
 MESH = pl.DeviceIdType.MESH
 F32 = jnp.float32
 BF16 = jnp.bfloat16
@@ -28,13 +28,14 @@
 
 def kernel(
     stream, down, router, expert, core, up, out,
-    w_down, w_router, w_expert, w_core, up_in, expert4, selector, unpack, ones,
-    h, square_own, square_in, logit_own, logit_in, proj_own, proj_in, reduced, mixing, ranked_own, ranked,
-    load_sem, up_send, up_recv, h_send, h_recv, square_send, square_recv, logit_send, logit_recv,
-    proj_send, proj_recv, reduced_send, reduced_recv, mixing_send, mixing_recv, ranked_send, ranked_recv, out_sem,
+    w_down, w_router, w_expert, w_core, up_in, expert4, selector, spread, group, tile4, ones,
+    h, square_own, square_mid, square_sum, square_in, logit_own, logit_mid, logit_sum, logit_in,
+    proj_own, proj_mid, proj_sum, proj_in, reduced, mixing, ranked_own, ranked,
+    load_sem, up_send, up_recv, h_send, h_recv, first_send, first_recv, second_send, second_recv, reduced_send, reduced_recv, mixing_send, mixing_recv, ranked_send, ranked_recv, out_sem,
 ):
     me = lax.axis_index("tensor")
     section = lax.axis_index("section")
+    my_y, my_x = me // 4, lax.rem(me, 4)
     sections = lax.axis_size("section")
     after = lax.rem(section + 1, sections)
     before = lax.rem(section + sections - 1, sections)
@@ -62,8 +63,13 @@
     selector[...] = jnp.where(columns // EX == rows, 1.0, 0.0).astype(BF16)
     rows = lax.broadcasted_iota(jnp.int32, (128, 128), 0)
     columns = lax.broadcasted_iota(jnp.int32, (128, 128), 1)
-    for g in range(G):
-        unpack[g] = jnp.where(rows == g * EX + columns % EX, 1.0, 0.0).astype(BF16)
+    tile4[...] = jnp.where(rows % EX == columns % EX, 1.0, 0.0).astype(BF16)
+    rows = lax.broadcasted_iota(jnp.int32, (T, NT * RP), 0)
+    columns = lax.broadcasted_iota(jnp.int32, (T, NT * RP), 1)
+    spread[...] = jnp.where((rows // TB == columns // RP) & (rows % RP == columns % RP), 1.0, 0.0).astype(BF16)
+    rows = lax.broadcasted_iota(jnp.int32, (T, 128), 0)
+    columns = lax.broadcasted_iota(jnp.int32, (T, 128), 1)
+    group[...] = jnp.where((rows % TB) // RP == columns // EX, 1.0, 0.0)
 
     for copy in loads:
         copy.wait()
@@ -91,73 +97,104 @@
                 source(d, peer), target(d), send, recv, device_id={"tensor": peer}, device_id_type=MESH
             ).start()
 
+    def along(axis, source, target, send, recv):
+        for d in range(1, 4):
+            if axis == "x":
+                place = lax.rem(my_x + d, 4)
+                peer = my_y * 4 + place
+            else:
+                place = lax.rem(my_y + d, 4)
+                peer = place * 4 + my_x
+            pltpu.make_async_remote_copy(
+                source(place), target(d - 1), send, recv, device_id={"tensor": peer}, device_id_type=MESH
+            ).start()
+
     def wait_bytes(ref, sem):
         pltpu.make_async_copy(ref, ref, sem).wait()
 
+    def sums_sent(c):
+        wait_bytes(square_mid.at[0, c], first_send.at[0, c])
+        wait_bytes(logit_mid.at[0, c], first_send.at[1, c])
+        wait_bytes(proj_mid.at[0, c], first_send.at[2, c])
+        wait_bytes(square_in.at[0, c], second_send.at[0, c])
+        wait_bytes(logit_in.at[0, c], second_send.at[1, c])
+        wait_bytes(proj_in.at[0, c], second_send.at[2, c])
+
     def project(k, c, lap):
         x = h[k, c]
 
         @pl.when(k > 0)
         def _():
-            wait_bytes(square_in.at[0, c], square_send.at[c])
-            wait_bytes(logit_own.at[c, pl.ds(0, NT - 1)], logit_send.at[c])
-            wait_bytes(proj_own.at[c, pl.ds(0, NT - 1)], proj_send.at[c])
+            sums_sent(c)
 
         squares = lax.dot_general(ones[...], (x * x).astype(BF16), NT_DIMS, preferred_element_type=F32)
         square_own[c] = squares[0:1]
-        to_peers(lambda d, p: square_own.at[c], lambda d: square_in.at[k, c, d - 1], square_send.at[c], square_recv.at[k, c])
+        along("x", lambda p: square_own.at[c], lambda d: square_mid.at[k, c, d], first_send.at[0, c], first_recv.at[0, k, c])
         low = x.astype(BF16)
-        part = jnp.dot(low, w_router[lap, 0], preferred_element_type=F32)
-        logit_own[c] = part.astype(BF16).reshape(NT, TB, RANK)
-        to_peers(lambda d, p: logit_own.at[c, p], lambda d: logit_in.at[k, c, d - 1], logit_send.at[c], logit_recv.at[k, c])
-        part = jnp.dot(low, w_down[lap, 0], preferred_element_type=F32)
-        proj_own[c] = part.astype(BF16).reshape(NT, TB, RANK)
-        to_peers(lambda d, p: proj_own.at[c, p], lambda d: proj_in.at[k, c, d - 1], proj_send.at[c], proj_recv.at[k, c])
+        part = jnp.dot(low, w_router[lap, 0], preferred_element_type=F32).reshape(4, 4, TB, RANK)
+        for i in range(4):
+            logit_own[c, i] = part[:, i].astype(BF16)
+        along("x", lambda p: logit_own.at[c, p], lambda d: logit_mid.at[k, c, d], first_send.at[1, c], first_recv.at[1, k, c])
+        part = jnp.dot(low, w_down[lap, 0], preferred_element_type=F32).reshape(4, 4, TB, RANK)
+        for i in range(4):
+            proj_own[c, i] = part[i].astype(BF16)
+        along("y", lambda p: proj_own.at[c, p], lambda d: proj_mid.at[k, c, d], first_send.at[2, c], first_recv.at[2, k, c])
+
+    def summed(own, arrived):
+        total = own.astype(F32)
+        for d in range(3):
+            total = total + arrived[d].astype(F32)
+        return total
+
+    def middle(k, c):
+        wait_bytes(square_mid.at[k, c], first_recv.at[0, k, c])
+        square_sum[c] = summed(square_own[c], square_mid.at[k, c])
+        along("y", lambda p: square_sum.at[c], lambda d: square_in.at[k, c, d], second_send.at[0, c], second_recv.at[0, k, c])
+        wait_bytes(logit_mid.at[k, c], first_recv.at[1, k, c])
+        logit_sum[c] = summed(logit_own[c, my_x], logit_mid.at[k, c]).astype(BF16)
+        along("y", lambda p: logit_sum.at[c, p], lambda d: logit_in.at[k, c, d], second_send.at[1, c], second_recv.at[1, k, c])
+        wait_bytes(proj_mid.at[k, c], first_recv.at[2, k, c])
+        proj_sum[c] = summed(proj_own[c, my_y], proj_mid.at[k, c]).astype(BF16)
+        along("x", lambda p: proj_sum.at[c, p], lambda d: proj_in.at[k, c, d], second_send.at[2, c], second_recv.at[2, k, c])
 
     def finish(k, c, lap):
-        wait_bytes(square_in.at[k, c], square_recv.at[k, c])
-        total = square_own[c]
-        for d in range(NT - 1):
-            total = total + square_in[k, c, d]
+        wait_bytes(square_in.at[k, c], second_recv.at[0, k, c])
+        total = summed(square_sum[c], square_in.at[k, c])
         at = lax.broadcasted_iota(jnp.int32, (TB, T), 1) == me * TB + lax.broadcasted_iota(jnp.int32, (TB, T), 0)
         own = jnp.sum(jnp.where(at, jnp.broadcast_to(total, (TB, T)), 0.0), axis=1, keepdims=True)
         factor = lax.rsqrt(own / D + EPSILON)
 
-        wait_bytes(logit_in.at[k, c], logit_recv.at[k, c])
-        logits = logit_own[c, me].astype(F32)
-        for d in range(NT - 1):
-            logits = logits + logit_in[k, c, d].astype(F32)
+        wait_bytes(logit_in.at[k, c], second_recv.at[1, k, c])
+        logits = summed(logit_sum[c, my_y], logit_in.at[k, c])
         gating = jax.nn.sigmoid(logits * factor).astype(BF16)
         mixed = jnp.dot(gating, expert4[lap], preferred_element_type=F32)
         mixed = mixed.astype(BF16).astype(F32)
-        lane = lax.broadcasted_iota(jnp.int32, (8, 128), 1) // EX
-        packed = jnp.zeros((8, 128), F32)
-        for g in range(G):
-            packed = jnp.where(lane == g, mixed[g * 8 : g * 8 + 8], packed)
+        lane = lax.broadcasted_iota(jnp.int32, (RP, 128), 1) // EX
+        packed = mixed[0:RP]
+        for g in range(1, 4):
+            packed = jnp.where(lane == g, mixed[g * RP : g * RP + RP], packed)
         mixing[k, c, me] = packed
         to_peers(lambda d, p: mixing.at[k, c, me], lambda d: mixing.at[k, c, me], mixing_send.at[c], mixing_recv.at[k, c])
 
-        wait_bytes(proj_in.at[k, c], proj_recv.at[k, c])
-        projected = proj_own[c, me].astype(F32)
-        for d in range(NT - 1):
-            projected = projected + proj_in[k, c, d].astype(F32)
+        wait_bytes(proj_in.at[k, c], second_recv.at[2, k, c])
+        projected = summed(proj_sum[c, my_x], proj_in.at[k, c])
         reduced[k, c, me] = (projected * factor).astype(BF16)
         to_peers(lambda d, p: reduced.at[k, c, me], lambda d: reduced.at[k, c, me], reduced_send.at[c], reduced_recv.at[k, c])
 
     def core_stage(k, c, lap):
         wait_bytes(mixing.at[k, c, pl.ds(0, NT - 1)], mixing_recv.at[k, c])
-        packed = mixing[k, c].reshape(128, 128).astype(BF16)
+        packed = mixing[k, c].reshape(NT * RP, 128).astype(BF16)
+        weights = jnp.dot(spread[...], packed, preferred_element_type=F32) * group[...]
+        weights = jnp.dot(weights.astype(BF16), tile4[...], preferred_element_type=F32)
         wait_bytes(reduced.at[k, c, pl.ds(0, NT - 1)], reduced_recv.at[k, c])
+        every = reduced[k, c].astype(F32).reshape(T, RANK).astype(BF16)
         part = lax.dot_general(
-            reduced[k, c].reshape(T, RANK), w_core[lap, 0].reshape(FB * EX, RANK), NT_DIMS, preferred_element_type=F32
-        ).reshape(NT, G, 8, FB * EX)
-        for g in range(G):
-            weights = jnp.dot(packed, unpack[g], preferred_element_type=F32).reshape(NT, 8, 128)
-            weights = jnp.concatenate([weights] * (FB * EX // 128), axis=2)
-            product = (part[:, g] * weights).reshape(128, FB * EX).astype(BF16)
-            ranked_own[k, c, :, g * 128 : g * 128 + 128] = lax.dot_general(
-                selector[...], product, NT_DIMS, preferred_element_type=F32
-            ).astype(BF16)
+            every, w_core[lap, 0].reshape(FB * EX, RANK), NT_DIMS, preferred_element_type=F32
+        )
+        product = (part * jnp.concatenate([weights] * (FB * EX // 128), axis=1)).astype(BF16)
+        ranked_own[k, c] = lax.dot_general(
+            selector[...], product, NT_DIMS, preferred_element_type=F32
+        ).astype(BF16)
         for d in range(NT):
             pltpu.make_async_remote_copy(
                 ranked_own.at[k, c], ranked.at[k, c, me], ranked_send.at[c], ranked_recv.at[k, c],
@@ -170,11 +207,7 @@
         update = lax.dot_general(
             ranked[k, c].reshape(RANK, T), up_in[lap, 0], TN_DIMS, preferred_element_type=F32
         )
-        update = update.reshape(G, NT, 8, 512)
-        for g in range(G):
-            rows = h[k + 1, c].reshape(NT, G, 8, 512)[:, g] + update[g]
-            for j in range(NT):
-                h[k + 1, c, (j * G + g) * 8 : (j * G + g) * 8 + 8] = rows[j]
+        h[k + 1, c] = h[k + 1, c] + update
 
     def hand_on(k, c):
         pltpu.make_async_remote_copy(
@@ -205,6 +238,8 @@
         def _():
             hand_up(1 - lap_of(section, 0))
 
+        for c in range(C):
+            middle(k, c)
         for c in range(C):
             finish(k, c, lap)
         for c in range(C):
@@ -218,9 +253,7 @@
         copies.append(pltpu.make_async_copy(h.at[TICKS, c], out.at[0, pl.ds(c * T, T)], out_sem.at[c]))
         copies[-1].start()
     for c in range(C):
-        wait_bytes(square_in.at[0, c], square_send.at[c])
-        wait_bytes(logit_own.at[c, pl.ds(0, NT - 1)], logit_send.at[c])
-        wait_bytes(proj_own.at[c, pl.ds(0, NT - 1)], proj_send.at[c])
+        sums_sent(c)
         wait_bytes(mixing.at[:, c, pl.ds(0, NT - 1)], mixing_send.at[c])
         wait_bytes(reduced.at[:, c, pl.ds(0, NT - 1)], reduced_send.at[c])
         wait_bytes(ranked.at[:, c], ranked_send.at[c])
@@ -247,17 +280,25 @@
             pltpu.VMEM(up_factor.shape, BF16),
             pltpu.VMEM((2, RANK, 128), BF16),
             pltpu.VMEM((FB, FB * EX), BF16),
-            pltpu.VMEM((G, 128, 128), BF16),
+            pltpu.VMEM((T, NT * RP), BF16),
+            pltpu.VMEM((T, 128), F32),
+            pltpu.VMEM((128, 128), BF16),
             pltpu.VMEM((8, MB), BF16),
             pltpu.VMEM((TICKS + 1, C, T, 512), F32),
             pltpu.VMEM((C, 1, T), F32),
-            pltpu.VMEM((TICKS, C, NT - 1, 1, T), F32),
-            pltpu.VMEM((C, NT, TB, RANK), BF16),
-            pltpu.VMEM((TICKS, C, NT - 1, TB, RANK), BF16),
-            pltpu.VMEM((C, NT, TB, RANK), BF16),
-            pltpu.VMEM((TICKS, C, NT - 1, TB, RANK), BF16),
+            pltpu.VMEM((TICKS, C, 3, 1, T), F32),
+            pltpu.VMEM((C, 1, T), F32),
+            pltpu.VMEM((TICKS, C, 3, 1, T), F32),
+            pltpu.VMEM((C, 4, 4, TB, RANK), BF16),
+            pltpu.VMEM((TICKS, C, 3, 4, TB, RANK), BF16),
+            pltpu.VMEM((C, 4, TB, RANK), BF16),
+            pltpu.VMEM((TICKS, C, 3, TB, RANK), BF16),
+            pltpu.VMEM((C, 4, 4, TB, RANK), BF16),
+            pltpu.VMEM((TICKS, C, 3, 4, TB, RANK), BF16),
+            pltpu.VMEM((C, 4, TB, RANK), BF16),
+            pltpu.VMEM((TICKS, C, 3, TB, RANK), BF16),
             pltpu.VMEM((TICKS, C, NT, TB, RANK), BF16),
-            pltpu.VMEM((TICKS, C, NT, 8, 128), F32),
+            pltpu.VMEM((TICKS, C, NT, RP, 128), F32),
             pltpu.VMEM((TICKS, C, FB, T), BF16),
             pltpu.VMEM((TICKS, C, NT, FB, T), BF16),
             dma((C + 4,)),
@@ -265,12 +306,10 @@
             dma((2,)),
             dma((C,)),
             dma((TICKS + 1, C)),
-            dma((C,)),
-            dma((TICKS, C)),
-            dma((C,)),
-            dma((TICKS, C)),
-            dma((C,)),
-            dma((TICKS, C)),
+            dma((3, C)),
+            dma((3, TICKS, C)),
+            dma((3, C)),
+            dma((3, TICKS, C)),
             dma((C,)),
             dma((TICKS, C)),
             dma((C,)),

time: 181 us -> 159 us (0.88); the launches traced: 181 us -> 156 us
  Pallas kernels: 177 us -> 152 us
    pallas_call x1, Pallas kernels: 177 us -> 152 us  [per_device(): pl.pallas_call(kernel, out_shape=jax.ShapeDtypeStruct(stream.shape, F32),...]
where the time goes in v3:
time: 159 us; the launch traced here: 156 us
  Pallas kernels  152 us (96%)
  local copies, waits for them, and re-layouts  3.94 us (2%)
    pallas_call x1, Pallas kernels, per_device(): pl.pallas_call(kernel, out_shape=jax.ShapeDtypeStruct(stream.shape, F32),...  152 us
    unnamed x2, local copies, waits for them, and re-layouts  3.94 us

profile of v3, /device:TPU:1, one launch (start us, length us, event | category | flops | bytes accessed | tf_op | source)
XLA Modules:
  0.0 156.1 jit_solution(9219602898345292055)
XLA Ops:
  0.0 1.7 %copy.7.expert = bf16[2,1,512,32]{3,2,1,0:T(8,128)(2,1)} copy(bf16[2,1,512,32]{2,3,1,0:T(8,128)(2,1)} %param.9) | data formatting | bytes 131072 | tf_op args[3]
  1.7 152.1 %relay_window.1 = f32[1,512,512]{2,1,0:T(8,128)} custom-call(f32[1,512,512]{2,1,0:T(8,128)} %stream.1, bf16[2,1,512,512]{3,2,1,0:T(8,128)(2,1)} %down.1, bf16[2,1,512,512]{3,2,1,0:T(8,128)(2,1)} %router.1, bf16[2,1,512,32]{3,2,1,0:T(8,128)(2,1)} %copy.7.expert, bf16[2,1,32,32,512]{4,3,2,1,0:T(8,128)(2,1)} %core.1, bf16[2,1,512,512]{3,2,1,0:T(8,128)(2,1)} %up.1), custom_call_target="tpu_custom_call" | custom-call | tf_op jit(solution)/shard_map/relay_window/pallas_call | solution.py:270
  153.8 2.3 %copy.9 = f32[1,512,512]{2,1,0:T(8,128)} copy(f32[1,512,512]{2,1,0:T(8,128)} %relay_window.1) | data formatting | bytes 2097152

commit v4 on v3

--- a/solution.py
+++ b/solution.py
@@ -71,11 +71,8 @@
     columns = lax.broadcasted_iota(jnp.int32, (T, 128), 1)
     group[...] = jnp.where((rows % TB) // RP == columns // EX, 1.0, 0.0)
 
-    for copy in loads:
+    for copy in loads[: C + 2]:
         copy.wait()
-    for lap in range(2):
-        one = w_expert[lap, 0]
-        expert4[lap] = jnp.concatenate([one, one, one, one], axis=1)
 
     pl.semaphore_wait(barrier, 2 * NT - 1)
 
@@ -127,9 +124,6 @@
         def _():
             sums_sent(c)
 
-        squares = lax.dot_general(ones[...], (x * x).astype(BF16), NT_DIMS, preferred_element_type=F32)
-        square_own[c] = squares[0:1]
-        along("x", lambda p: square_own.at[c], lambda d: square_mid.at[k, c, d], first_send.at[0, c], first_recv.at[0, k, c])
         low = x.astype(BF16)
         part = jnp.dot(low, w_router[lap, 0], preferred_element_type=F32).reshape(4, 4, TB, RANK)
         for i in range(4):
@@ -139,6 +133,9 @@
         for i in range(4):
             proj_own[c, i] = part[i].astype(BF16)
         along("y", lambda p: proj_own.at[c, p], lambda d: proj_mid.at[k, c, d], first_send.at[2, c], first_recv.at[2, k, c])
+        squares = lax.dot_general(ones[...], (x * x).astype(BF16), NT_DIMS, preferred_element_type=F32)
+        square_own[c] = squares[0:1]
+        along("x", lambda p: square_own.at[c], lambda d: square_mid.at[k, c, d], first_send.at[0, c], first_recv.at[0, k, c])
 
     def summed(own, arrived):
         total = own.astype(F32)
@@ -158,6 +155,10 @@
         along("x", lambda p: proj_sum.at[c, p], lambda d: proj_in.at[k, c, d], second_send.at[2, c], second_recv.at[2, k, c])
 
     def finish(k, c, lap):
+        wait_bytes(proj_in.at[k, c], second_recv.at[2, k, c])
+        projected = summed(proj_sum[c, my_x], proj_in.at[k, c])
+        reduced[k, c, me] = projected.astype(BF16)
+        to_peers(lambda d, p: reduced.at[k, c, me], lambda d: reduced.at[k, c, me], reduced_send.at[c], reduced_recv.at[k, c])
         wait_bytes(square_in.at[k, c], second_recv.at[0, k, c])
         total = summed(square_sum[c], square_in.at[k, c])
         at = lax.broadcasted_iota(jnp.int32, (TB, T), 1) == me * TB + lax.broadcasted_iota(jnp.int32, (TB, T), 0)
@@ -167,30 +168,24 @@
         wait_bytes(logit_in.at[k, c], second_recv.at[1, k, c])
         logits = summed(logit_sum[c, my_y], logit_in.at[k, c])
         gating = jax.nn.sigmoid(logits * factor).astype(BF16)
-        mixed = jnp.dot(gating, expert4[lap], preferred_element_type=F32)
-        mixed = mixed.astype(BF16).astype(F32)
+        mixed = lax.dot_general(gating, expert4[lap], NT_DIMS, preferred_element_type=F32) * factor
         lane = lax.broadcasted_iota(jnp.int32, (RP, 128), 1) // EX
         packed = mixed[0:RP]
         for g in range(1, 4):
             packed = jnp.where(lane == g, mixed[g * RP : g * RP + RP], packed)
-        mixing[k, c, me] = packed
+        mixing[k, c, me] = packed.astype(BF16)
         to_peers(lambda d, p: mixing.at[k, c, me], lambda d: mixing.at[k, c, me], mixing_send.at[c], mixing_recv.at[k, c])
 
-        wait_bytes(proj_in.at[k, c], second_recv.at[2, k, c])
-        projected = summed(proj_sum[c, my_x], proj_in.at[k, c])
-        reduced[k, c, me] = (projected * factor).astype(BF16)
-        to_peers(lambda d, p: reduced.at[k, c, me], lambda d: reduced.at[k, c, me], reduced_send.at[c], reduced_recv.at[k, c])
-
     def core_stage(k, c, lap):
-        wait_bytes(mixing.at[k, c, pl.ds(0, NT - 1)], mixing_recv.at[k, c])
-        packed = mixing[k, c].reshape(NT * RP, 128).astype(BF16)
-        weights = jnp.dot(spread[...], packed, preferred_element_type=F32) * group[...]
-        weights = jnp.dot(weights.astype(BF16), tile4[...], preferred_element_type=F32)
         wait_bytes(reduced.at[k, c, pl.ds(0, NT - 1)], reduced_recv.at[k, c])
         every = reduced[k, c].astype(F32).reshape(T, RANK).astype(BF16)
         part = lax.dot_general(
             every, w_core[lap, 0].reshape(FB * EX, RANK), NT_DIMS, preferred_element_type=F32
         )
+        wait_bytes(mixing.at[k, c, pl.ds(0, NT - 1)], mixing_recv.at[k, c])
+        packed = mixing[k, c].astype(F32).reshape(NT * RP, 128).astype(BF16)
+        weights = jnp.dot(spread[...], packed, preferred_element_type=F32) * group[...]
+        weights = jnp.dot(weights.astype(BF16), tile4[...], preferred_element_type=F32)
         product = (part * jnp.concatenate([weights] * (FB * EX // 128), axis=1)).astype(BF16)
         ranked_own[k, c] = lax.dot_general(
             selector[...], product, NT_DIMS, preferred_element_type=F32
@@ -231,8 +226,8 @@
 
                 advance(k - 1, c, earlier)
 
+            project(k, c, lap)
             hand_on(k, c)
-            project(k, c, lap)
 
         @pl.when(k == 1)
         def _():
@@ -240,8 +235,20 @@
 
         for c in range(C):
             middle(k, c)
+        @pl.when(k == 0)
+        def _():
+            loads[C + 2].wait()
+            for i in range(2):
+                one = w_expert[i, 0]
+                expert4[i] = jnp.concatenate([one, one, one, one], axis=0)
+
         for c in range(C):
             finish(k, c, lap)
+
+        @pl.when(k == 0)
+        def _():
+            loads[C + 3].wait()
+
         for c in range(C):
             core_stage(k, c, lap)
         return carry
@@ -265,6 +272,7 @@
 
 
 def per_device(stream, down_factor, router, expert_factor, core_tensor, up_factor):
+    expert_factor = jnp.swapaxes(expert_factor, 2, 3)
     operands = (stream, down_factor, router, expert_factor, core_tensor, up_factor)
     dma = pltpu.SemaphoreType.DMA
     return pl.pallas_call(
@@ -278,7 +286,7 @@
             pltpu.VMEM(expert_factor.shape, BF16),
             pltpu.VMEM(core_tensor.shape, BF16),
             pltpu.VMEM(up_factor.shape, BF16),
-            pltpu.VMEM((2, RANK, 128), BF16),
+            pltpu.VMEM((2, 128, RANK), BF16),
             pltpu.VMEM((FB, FB * EX), BF16),
             pltpu.VMEM((T, NT * RP), BF16),
             pltpu.VMEM((T, 128), F32),
@@ -298,7 +306,7 @@
             pltpu.VMEM((C, 4, TB, RANK), BF16),
             pltpu.VMEM((TICKS, C, 3, TB, RANK), BF16),
             pltpu.VMEM((TICKS, C, NT, TB, RANK), BF16),
-            pltpu.VMEM((TICKS, C, NT, RP, 128), F32),
+            pltpu.VMEM((TICKS, C, NT, RP, 128), BF16),
             pltpu.VMEM((TICKS, C, FB, T), BF16),
             pltpu.VMEM((TICKS, C, NT, FB, T), BF16),
             dma((C + 4,)),

time: 159 us -> 156 us (0.981)
  local copies, waits for them, and re-layouts: 3.94 us -> 2.26 us
    unnamed x2 -> x1, local copies, waits for them, and re-layouts: 3.94 us -> 2.26 us
where the time goes in v4:
time: 156 us; the launch traced here: 153 us
  Pallas kernels  151 us (97%)
  local copies, waits for them, and re-layouts  2.26 us (1%)
    pallas_call x1, Pallas kernels, per_device(): pl.pallas_call(kernel, out_shape=jax.ShapeDtypeStruct(stream.shape, F32),...  151 us

profile of v4, /device:TPU:1, one launch (start us, length us, event | category | flops | bytes accessed | tf_op | source)
XLA Modules:
  0.0 153.1 jit_solution(14538830494086428308)
XLA Ops:
  0.0 150.9 %relay_window.1 = f32[1,512,512]{2,1,0:T(8,128)} custom-call(f32[1,512,512]{2,1,0:T(8,128)} %stream.1, bf16[2,1,512,512]{3,2,1,0:T(8,128)(2,1)} %down.1, bf16[2,1,512,512]{3,2,1,0:T(8,128)(2,1)} %router.1, bf16[2,1,32,512]{3,2,1,0:T(8,128)(2,1)} %bitcast.1, bf16[2,1,32,32,512]{4,3,2,1,0:T(8,128)(2,1)} %core.1, bf16[2,1,512,512]{3,2,1,0:T(8,128)(2,1)} %up.1), custom_call_target="tpu_custom_call" | custom-call | tf_op jit(solution)/shard_map/relay_window/pallas_call | solution.py:278
  150.9 2.3 %copy.8 = f32[1,512,512]{2,1,0:T(8,128)} copy(f32[1,512,512]{2,1,0:T(8,128)} %relay_window.1) | data formatting | bytes 2097152

commit v5 on v4

--- a/solution.py
+++ b/solution.py
@@ -19,6 +19,9 @@
 T = MB // C
 TB = T // NT
 RP = TB // 4
+FAR_FIRST = sorted(
+    ((dy, dx) for dy in range(4) for dx in range(4)), key=lambda o: -sum(min(v, 4 - v) for v in o)
+)
 MESH = pl.DeviceIdType.MESH
 F32 = jnp.float32
 BF16 = jnp.bfloat16
@@ -88,14 +91,14 @@
     hand_up(lap_of(section, 0))
 
     def to_peers(source, target, send, recv):
-        for d in range(1, NT):
-            peer = lax.rem(me + d, NT)
+        for dy, dx in FAR_FIRST[:-1]:
+            peer = lax.rem(my_y + dy, 4) * 4 + lax.rem(my_x + dx, 4)
             pltpu.make_async_remote_copy(
-                source(d, peer), target(d), send, recv, device_id={"tensor": peer}, device_id_type=MESH
+                source(peer), target(), send, recv, device_id={"tensor": peer}, device_id_type=MESH
             ).start()
 
     def along(axis, source, target, send, recv):
-        for d in range(1, 4):
+        for d in (2, 1, 3):
             if axis == "x":
                 place = lax.rem(my_x + d, 4)
                 peer = my_y * 4 + place
@@ -158,7 +161,7 @@
         wait_bytes(proj_in.at[k, c], second_recv.at[2, k, c])
         projected = summed(proj_sum[c, my_x], proj_in.at[k, c])
         reduced[k, c, me] = projected.astype(BF16)
-        to_peers(lambda d, p: reduced.at[k, c, me], lambda d: reduced.at[k, c, me], reduced_send.at[c], reduced_recv.at[k, c])
+        to_peers(lambda p: reduced.at[k, c, me], lambda: reduced.at[k, c, me], reduced_send.at[c], reduced_recv.at[k, c])
         wait_bytes(square_in.at[k, c], second_recv.at[0, k, c])
         total = summed(square_sum[c], square_in.at[k, c])
         at = lax.broadcasted_iota(jnp.int32, (TB, T), 1) == me * TB + lax.broadcasted_iota(jnp.int32, (TB, T), 0)
@@ -174,7 +177,7 @@
         for g in range(1, 4):
             packed = jnp.where(lane == g, mixed[g * RP : g * RP + RP], packed)
         mixing[k, c, me] = packed.astype(BF16)
-        to_peers(lambda d, p: mixing.at[k, c, me], lambda d: mixing.at[k, c, me], mixing_send.at[c], mixing_recv.at[k, c])
+        to_peers(lambda p: mixing.at[k, c, me], lambda: mixing.at[k, c, me], mixing_send.at[c], mixing_recv.at[k, c])
 
     def core_stage(k, c, lap):
         wait_bytes(reduced.at[k, c, pl.ds(0, NT - 1)], reduced_recv.at[k, c])
@@ -190,10 +193,11 @@
         ranked_own[k, c] = lax.dot_general(
             selector[...], product, NT_DIMS, preferred_element_type=F32
         ).astype(BF16)
-        for d in range(NT):
+        for dy, dx in FAR_FIRST:
+            peer = lax.rem(my_y + dy, 4) * 4 + lax.rem(my_x + dx, 4)
             pltpu.make_async_remote_copy(
                 ranked_own.at[k, c], ranked.at[k, c, me], ranked_send.at[c], ranked_recv.at[k, c],
-                device_id={"section": after, "tensor": lax.rem(me + d, NT)}, device_id_type=MESH,
+                device_id={"section": after, "tensor": peer}, device_id_type=MESH,
             ).start()
 
     def advance(k, c, lap):

time: 156 us -> 154 us (0.987)
  Pallas kernels: 151 us -> 149 us
    pallas_call x1, Pallas kernels: 151 us -> 149 us  [per_device(): pl.pallas_call(kernel, out_shape=jax.ShapeDtypeStruct(stream.shape, F32),...]
where the time goes in v5:
time: 154 us; the launch traced here: 151 us
  Pallas kernels  149 us (97%)
  local copies, waits for them, and re-layouts  2.26 us (1%)
    pallas_call x1, Pallas kernels, per_device(): pl.pallas_call(kernel, out_shape=jax.ShapeDtypeStruct(stream.shape, F32),...  149 us

profile of v5, /device:TPU:1, one launch (start us, length us, event | category | flops | bytes accessed | tf_op | source)
XLA Modules:
  0.0 151.5 jit_solution(7269705655799886843)
XLA Ops:
  0.0 149.2 %relay_window.1 = f32[1,512,512]{2,1,0:T(8,128)} custom-call(f32[1,512,512]{2,1,0:T(8,128)} %stream.1, bf16[2,1,512,512]{3,2,1,0:T(8,128)(2,1)} %down.1, bf16[2,1,512,512]{3,2,1,0:T(8,128)(2,1)} %router.1, bf16[2,1,32,512]{3,2,1,0:T(8,128)(2,1)} %bitcast.1, bf16[2,1,32,32,512]{4,3,2,1,0:T(8,128)(2,1)} %core.1, bf16[2,1,512,512]{3,2,1,0:T(8,128)(2,1)} %up.1), custom_call_target="tpu_custom_call" | custom-call | tf_op jit(solution)/shard_map/relay_window/pallas_call | solution.py:282
  149.2 2.3 %copy.8 = f32[1,512,512]{2,1,0:T(8,128)} copy(f32[1,512,512]{2,1,0:T(8,128)} %relay_window.1) | data formatting | bytes 2097152
